TPU v7x, 32 devices: a whole 2x2x4 slice. The times are simulated.
32 devices in a mesh: dp: 8 (over z, y), tensor: 4 (over x, core).
Axes of the slice: x: 2, y: 2, z: 4, core: 2. Of those that a mesh axis runs over, the one named last changes fastest.
Arguments:
- inputs: bfloat16 [16, 1024, 512], P('dp', 'tensor'), may hold values from -6 to 6
- memory: bfloat16 [16, 1024, 512], P('dp', 'tensor'), may hold values from -6 to 6
- tgt_len: int32 [16], P('dp'), may hold values from 512 to 1024, as said below
- src_len: int32 [16], P('dp'), may hold values from 512 to 1024, as said below
- cotangent: bfloat16 [16, 1024, 512], P('dp', 'tensor'), may hold values from -6 to 6
- w_qkv: bfloat16 [3, 512, 512], P(None, 'dp', 'tensor'), may hold values from -0.25 to 0.25
- w_out: bfloat16 [512, 512], P('tensor', 'dp'), may hold values from -6 to 6
- cross_query: bfloat16 [512, 512], P('dp', 'tensor'), may hold values from -0.25 to 0.25
- cross_kv: bfloat16 [2, 512, 512], P(None, 'dp', 'tensor'), may hold values from -0.25 to 0.25
- cross_out: bfloat16 [512, 512], P('tensor', 'dp'), may hold values from -6 to 6
- ffn_up: bfloat16 [512, 2048], P('dp', 'tensor'), may hold values from -0.25 to 0.25
- ffn_down: bfloat16 [2048, 512], P('tensor', 'dp'), may hold values from -0.1875 to 0.1875
- gain_one: bfloat16 [512], P('dp'), may hold values from 0.099609375 to 1.8984375
- bias_one: bfloat16 [512], P('dp'), may hold values from -3 to 3
- gain_two: bfloat16 [512], P('dp'), may hold values from 0.099609375 to 1.8984375
- bias_two: bfloat16 [512], P('dp'), may hold values from -3 to 3
- gain_three: bfloat16 [512], P('dp'), may hold values from 0.099609375 to 1.8984375
- bias_three: bfloat16 [512], P('dp'), may hold values from -3 to 3
Outputs:
- output: bfloat16 [16, 1024, 512], P('dp', 'tensor')
- grad_inputs: float32 [16, 1024, 512], P('dp', 'tensor')
- grad_memory: float32 [16, 1024, 512], P('dp', 'tensor')
- grad_w_qkv: float32 [3, 512, 512], P(None, 'dp', 'tensor')
- grad_w_out: float32 [512, 512], P('tensor', 'dp')
- grad_cross_query: float32 [512, 512], P('dp', 'tensor')
- grad_cross_kv: float32 [2, 512, 512], P(None, 'dp', 'tensor')
- grad_cross_out: float32 [512, 512], P('tensor', 'dp')
- grad_ffn_up: float32 [512, 2048], P('dp', 'tensor')
- grad_ffn_down: float32 [2048, 512], P('tensor', 'dp')
- grad_gain_one: float32 [512], P('dp')
- grad_bias_one: float32 [512], P('dp')
- grad_gain_two: float32 [512], P('dp')
- grad_bias_two: float32 [512], P('dp')
- grad_gain_three: float32 [512], P('dp')
- grad_bias_three: float32 [512], P('dp')
Inputs may be any that keep to these rules, and one draw needn't show every extreme that they name: `tgt_len`: one sequence has a target length of 1024 and another of 512. `src_len`: one sequence has a source length of 1024 and another of 512.
All inputs are finite; a program needn't handle non-finite values.
Results may differ from a plain program's by a relative error of at most 0.015.
Values may be sent and summed in bfloat16 or wider, within the bound.
A program may use at most 128 MiB of HBM per device.

v0:
```python
import functools

import jax
import jax.numpy as jnp
from jax import lax
from jax.experimental import pallas as pl
from jax.experimental.pallas import tpu as pltpu
from jax.sharding import PartitionSpec as P

DH = 64
LANES = 128
EPSILON = 1e-05
MASKED = -1e30
F32 = jnp.float32
BF16 = jnp.bfloat16
MESH = pl.DeviceIdType.MESH
HIGHEST = lax.Precision.HIGHEST


def nn(a, b):
    return lax.dot_general(a, b, (((1,), (0,)), ((), ())), preferred_element_type=F32)


def nt(a, b):
    return lax.dot_general(a, b, (((1,), (1,)), ((), ())), preferred_element_type=F32)


def normalize(values):
    center = values - jnp.mean(values, axis=-1, keepdims=True)
    spread = jnp.mean(center * center, axis=-1, keepdims=True)
    inv = lax.rsqrt(spread + EPSILON)
    return center * inv, inv


def norm_grad(values, grad, gain):
    xhat, inv = normalize(values)
    e = grad * gain
    back = inv * (
        e
        - jnp.mean(e, axis=-1, keepdims=True)
        - xhat * jnp.mean(e * xhat, axis=-1, keepdims=True)
    )
    return (
        back,
        jnp.sum(grad * xhat, axis=0, keepdims=True),
        jnp.sum(grad, axis=0, keepdims=True),
    )


def gelu_both(v):
    c = 0.7978845608028654
    v2 = v * v
    t = jnp.tanh(v * (c + (c * 0.044715) * v2))
    half = 0.5 * (1.0 + t)
    slope = half + (0.5 * v) * (1.0 - t * t) * (c + (3.0 * c * 0.044715) * v2)
    return v * half, slope


ORDERS = {
    "A0": ("xzy",),
    "A1": ("yzx",),
    "A2": ("zyx",),
    "W": ("zxy", "zyx"),
    "K": ("zxy", "zyx"),
    "Q0": ("zxy", "zyx"),
    "Q1": ("zxy", "zyx"),
    "U0": ("yxz",),
    "U1": ("zxy",),
    "D0": ("zxy",),
    "D1": ("zyx",),
    "rD0": ("zxy",),
    "rD1": ("zxy",),
    "rU0": ("xzy",),
    "rU1": ("yxz",),
    "rco": ("yzx",),
    "rcq": ("xzy",),
    "rck": ("zxy",),
    "rwo": ("zxy",),
    "rT": ("xyz", "yzx"),
    "rG": ("yzx",),
}

PLAN = {
    "p0": ("A2", "x", "W", "A1", "gz", "A1", "A2", "A0", "W", "gz", "x", "A0", "A2", "A1", "gz"),
    "p1": ("K", "m", "U0", "A2", "A0", "Q0", "A1", "Q1", "U1", "K", "W", "D0", "A0"),
    "p2": ("Q0", "m", "Q1", "U0", "D1"),
    "p3": ("K",),
    "p4": ("W",),
    "p5": (),
    "p6": ("Q0", "Q1", "U0"),
    "p7": ("U1",),
    "p8": ("K", "D1"),
    "p9": ("Q0", "D0"),
    "p10": ("Q1",),
    "p11": ("U1", "c"),
    "p12": (),
    "p13": (),
    "p14": ("D0", "D1"),
    "p15": ("U0",),
    "p16": ("U1",),
    "p17": ("c",),
    "p18": (),
    "p19": ("rD1", "D0", "D1"),
    "p20": (),
    "p21": ("rU0", "rU1"),
    "p22": ("rD0",),
    "p23": ("out", "rco"),
    "p24": (),
    "p25": ("rD1", "rU1"),
    "p26": ("rD1", "out", "rU0"),
    "p27": ("rD1", "rD0", "rU1"),
    "p28": ("rcq", "rck"),
    "p29": ("rD0", "gm"),
    "p30": ("rU0",),
    "p31": ("rU0", "rD0", "rU1"),
    "p32": ("gm", "rwo"),
    "p33": (),
    "p34": (),
    "p35": ("rT", "rcq"),
    "p36": ("rco",),
    "p37": ("rG", "rwo", "gi", "rck", "rT", "rcq", "rwo", "rco", "rG", "rcq", "rwo", "gi", "rT", "rck", "rco", "rG", "rck", "rG", "rT"),
}


def gather_segments(nf):
    mid = 8 + nf // 2
    end = 8 + nf
    last = end + nf // 2
    return {
        "A0": (0, 1), "A1": (1, 2), "A2": (2, 3), "W": (3, 4), "K": (4, 6), "Q0": (6, 7),
        "Q1": (7, 8), "U0": (8, mid), "U1": (mid, end), "D0": (end, last),
        "D1": (last, end + nf),
    }


def sum_segments(nf):
    mid = 9 + nf // 2
    end = 9 + nf
    last = end + nf // 2
    return {
        "rT": (0, 3), "rwo": (3, 4), "rck": (4, 6), "rcq": (6, 7), "rco": (7, 8), "rG": (8, 9),
        "rU0": (9, mid), "rU1": (mid, end), "rD0": (end, last), "rD1": (last, end + nf),
    }


def sum_shapes(order, segs, nz, ny, rows):
    shapes, left = [], {"x": 2 * LANES, "y": (ny,), "z": (nz,)}
    for i, axis in enumerate(order):
        left[axis] = LANES if axis == "x" else ()
        shape = (segs, *left["z"], *left["y"], rows, left["x"])
        shapes.append((nz - 1, *shape) if axis == "z" else shape)
        if i < 2:
            shapes.append(shape)
    return shapes


def layer_kernel(cfg, *refs):
    fused, nz, ny, rb, own, wide, nf = cfg
    rows_all = 4 * own
    nseg = 8 + 2 * nf
    gseg = 8
    refs = list(refs)

    def take(count):
        got, refs[:count] = refs[:count], []
        return got

    x_ref, m_ref, c_ref, tl_ref, sl_ref = take(5)
    if fused:
        wqkv_ref, wo_ref, cq_ref, ckv_ref, co_ref, up_ref, dn_ref = take(7)
        gain_refs = take(6)
    else:
        wfull_ref, gfull_ref = take(2)
    out_ref, gi_ref, gm_ref, gw_ref = take(4)
    (xs, ms, cs, wg, gains, n1, n2, n3, h1, h2, gh, gb16, qs, ks, vs, cqs, cks, cvs,
     vt, smix, cmix, slse, clse, act, gbf, dm, dq, dk, dv, ps, pr, ys, yr,
     us, ur, outs, osend, gis, gisend, gms, gmsend, gs, bias, gacc, score) = take(45)
    if fused:
        gz, gy = take(2)
        sums = {name: [take(5) for _ in ORDERS[name]] for name in sum_segments(nf)}
    ssem, rsem, xss, xrs, lsem = take(5)

    p = lax.axis_index("tensor") // 2
    c = lax.axis_index("tensor") % 2
    t = 2 * p + c
    tx = 2 * (1 - p) + c
    dp_at = lax.axis_index("dp")
    core_peer = {"dp": dp_at, "tensor": 2 * p + 1 - c}
    x_peer = {"dp": dp_at, "tensor": tx}
    z = dp_at // ny
    y = dp_at % ny
    y_peer = {"dp": z * ny + (1 - y), "tensor": t}

    y_other, p_other = 1 - y, 1 - p
    z_others = [(z + k) % nz for k in range(1, nz)]
    z_peers = [{"dp": at_z * ny + y, "tensor": t} for at_z in z_others]

    def z_peer(k):
        return z_peers[k - 1]

    counter = [0]
    sent = []

    def view(pair):
        ref, index = pair
        return ref if index is None else ref.at[index]

    class Sent:
        def __init__(self, src, dst, peer):
            self.parts = src, dst, peer, counter[0]
            counter[0] += 1

        def copy(self):
            src, dst, peer, i = self.parts
            return pltpu.make_async_remote_copy(
                view(src), view(dst), ssem.at[i], rsem.at[i],
                device_id=peer, device_id_type=MESH,
            )

        def wait_recv(self):
            self.copy().wait_recv()

    class Kept:
        def __init__(self, src, dst):
            self.parts = src, dst, lcount[0]
            lcount[0] += 1

        def copy(self):
            src, dst, i = self.parts
            return pltpu.make_async_copy(view(src), view(dst), lsem.at[i])

        def wait(self):
            self.copy().wait()

    def push(src, dst, peer):
        cp = Sent(src, dst, peer)
        cp.copy().start()
        sent.append(cp)
        return cp

    lcount = [0]

    def local(src, dst):
        cp = Kept(src, dst)
        cp.copy().start()
        return cp

    def rows(j, size=own):
        return pl.ds(pl.multiple_of(j * size, size), size)

    peers = [core_peer, x_peer]
    if fused:
        peers.append(y_peer)
        peers += [z_peer(k) for k in range(1, nz)]
    rows_t, rows_tx = rows(t), rows(tx)
    barrier = pltpu.get_barrier_semaphore()
    for peer in peers:
        pl.semaphore_signal(barrier, inc=1, device_id=peer, device_id_type=MESH)

    half = pl.ds(pl.multiple_of(p * LANES, LANES), LANES)
    other_half = pl.ds(pl.multiple_of((1 - p) * LANES, LANES), LANES)

    if fused:
        own_part = [wqkv_ref[...], wo_ref[...][None], ckv_ref[...], cq_ref[...][None]]
        own_part.append(co_ref[...][None])
        at = 0
        for piece in own_part:
            wg[at : at + piece.shape[0], z, y, :, half] = piece
            at += piece.shape[0]
        for i in range(nf):
            wg[8 + i, z, y, :, half] = up_ref[:, i * LANES : (i + 1) * LANES]
            wg[8 + nf + i, z, y, :, half] = dn_ref[:, i * LANES : (i + 1) * LANES]
        place = (
            lax.broadcasted_iota(jnp.int32, (rb, wide), 0) + dp_at * rb
            == lax.broadcasted_iota(jnp.int32, (rb, wide), 1)
        ).astype(BF16)
        gz[0] = jnp.zeros((16, wide), BF16)
        for i in range(6):
            gz[0, i : i + 1, :] = nn(gain_refs[i][...], place).astype(BF16)
    pl.semaphore_wait(barrier, len(peers))

    relays = {}

    def carry(name, src, buf):
        over = push((src, p_other), (buf, rows_t), x_peer)
        keep = local((src, p), (buf, rows_t))
        near = push((src, p), (buf, rows_t), core_peer)
        yield
        over.wait_recv()
        relays[name] = push((buf, rows_tx), (buf, rows_tx), core_peer)
        keep.wait()
        near.wait_recv()
        yield

    def back_over(src, buf):
        cp = push((src, None), (buf, p), x_peer)
        yield
        cp.wait_recv()
        yield

    tasks = {
        "x": [carry("x", x_ref, xs)],
        "m": [carry("m", m_ref, ms)],
        "c": [carry("c", c_ref, cs)],
        "out": [back_over(osend, outs)],
        "gm": [back_over(gmsend, gms)],
        "gi": [back_over(gisend, gis)],
        "gz": [],
    }

    def at(name):
        for task in PLAN[name]:
            for part in tasks[task]:
                next(part)

    def at_turn(i, turn, name):
        if PLAN[name]:

            @pl.when(i == turn)
            def _():
                at(name)

    def gather(lo, hi, first, last, order):
        r = slice(first, last)
        zi, yi, lanes = z, y, half
        hops = []
        for axis in order:
            for cp in hops:
                cp.wait_recv()
            part = (wg, (slice(lo, hi), zi, yi, r, lanes))
            if axis == "x":
                hops = [push(part, part, x_peer)]
                lanes = pl.ds(0, 2 * LANES)
            elif axis == "y":
                hops = [push(part, part, y_peer)]
                yi = slice(None)
            else:
                hops = [push(part, part, z_peer(k)) for k in range(1, nz)]
                zi = slice(None)
            yield
        for cp in hops:
            cp.wait_recv()
        yield

    def gain_rows():
        cps = [push((gz, 0), (gz, k), z_peer(k)) for k in range(1, nz)]
        yield
        for cp in cps:
            cp.wait_recv()
        total = gz[0].astype(F32)
        for k in range(1, nz):
            total = total + gz[k].astype(F32)
        gy[0] = total.astype(BF16)
        cp = push((gy, 0), (gy, 1), y_peer)
        yield
        cp.wait_recv()
        gains[...] = total + gy[1].astype(F32)
        yield

    for name, (lo, hi) in gather_segments(nf).items():
        size = rb // len(ORDERS[name])
        tasks[name] = [
            gather(lo, hi, i * size, (i + 1) * size, order)
            for i, order in enumerate(ORDERS[name])
            if fused
        ]
    if fused:
        tasks["gz"] = [gain_rows()]

    def weight(s):
        return wg[s].reshape(nz * ny * rb, 2 * LANES)

    if not fused:
        wcp = local((wfull_ref, None), (wg, None))
        gains[...] = gfull_ref[...]
    at("p0")
    relays["x"].wait_recv()
    if not fused:
        wcp.wait()

    sub = min(64, own)
    per = own // sub
    gacc[...] = jnp.zeros_like(gacc)

    def norm_rows(i, _):
        r = rows(i, sub)
        xhat, _unused = normalize(xs[r, :].astype(F32))
        n1[r, :] = (xhat * gains[0:1, :] + gains[1:2, :]).astype(BF16)
        return 0

    lax.fori_loop(0, 4 * per, norm_rows, 0)
    at("p1")

    def put_pairs(buf, r, value):
        v = value.astype(BF16)
        buf[0, r, :] = v[:, :LANES]
        buf[1, r, :] = v[:, LANES:]

    def pairs(buf, r):
        return jnp.concatenate([buf[0, r, :], buf[1, r, :]], axis=1)

    scale = DH ** (-0.5)

    def put_transposed(buf, r, value):
        vt_ = value.T.astype(BF16)
        buf[0, :, r] = vt_[:LANES]
        buf[1, :, r] = vt_[LANES:]

    def project(j, _):
        r = rows(j)
        rowsv = n1[r, :]
        put_pairs(qs, r, nn(rowsv, weight(0)).astype(BF16) * jnp.asarray(scale, BF16))
        put_pairs(ks, r, nn(rowsv, weight(1)))
        val = nn(rowsv, weight(2))
        put_pairs(vs, r, val)
        put_transposed(vt, r, val.astype(BF16).astype(F32))
        return 0

    lax.fori_loop(0, 4, project, 0)
    at("p2")


    lane_at = lax.broadcasted_iota(jnp.int32, (1, LANES), 1)
    head_lanes = [((lane_at // DH) == u).astype(F32).astype(BF16) for u in range(2)]

    def only(value, u):
        return value * head_lanes[u]

    wide_rows = 2 * own

    def qrows(jj):
        return pl.ds(pl.multiple_of(jj * wide_rows, wide_rows), wide_rows)

    def hide(scores, first, diagonal, causal):
        if causal and not diagonal:
            return scores
        if causal:
            key_at = lax.broadcasted_iota(jnp.int32, scores.shape, 0)
            query_at = lax.broadcasted_iota(jnp.int32, scores.shape, 1)
            return jnp.where(key_at <= query_at, scores, MASKED)
        b = bias[first : first + scores.shape[0], :]
        return scores + jnp.concatenate([b] * (wide_rows // LANES), axis=1)

    def attend(pp, q_s, k_s, v_t, mix, lse, r, keys, causal):
        parts_k = [slice(i * wide_rows, (i + 1) * wide_rows) for i in range(keys // wide_rows)]

        q = q_s[pp, r, :]
        tops = [None, None]
        for i, kk in enumerate(parts_k):
            for u in range(2):
                s = nt(only(k_s[pp, kk, :], u), q)
                s = hide(s, kk.start, i == len(parts_k) - 1, causal)
                top = jnp.max(s, axis=0, keepdims=True)
                tops[u] = top if i == 0 else jnp.maximum(tops[u], top)
                score[u, kk, :] = s
        totals, mixed = [None, None], [None, None]
        for i, kk in enumerate(parts_k):
            for u in range(2):
                e = jnp.exp(score[u, kk, :] - tops[u])
                total = jnp.sum(e, axis=0, keepdims=True)
                o = nn(v_t[pp, u * DH : (u + 1) * DH, kk], e.astype(BF16))
                totals[u] = total if i == 0 else totals[u] + total
                mixed[u] = o if i == 0 else mixed[u] + o
        for u in range(2):
            lse[2 * pp + u, :, r] = tops[u] + jnp.log(totals[u])
            mixed[u] = mixed[u] * (1.0 / totals[u])
        mix[pp, r, :] = jnp.concatenate(mixed, axis=0).T.astype(BF16)

    def exchange(point, j):
        b = point % 2
        i = point * 4 + j
        return pltpu.make_async_remote_copy(
            ps.at[b, rows(j)], pr.at[b, rows(j)], xss.at[i], xrs.at[i],
            device_id=core_peer, device_id_type=MESH,
        )

    def send_sum(point, j, value):
        ps[point % 2, rows(j), :] = value.astype(BF16)
        exchange(point, j).start()

    def summed(point, r):
        b = point % 2
        return ps[b, r, :].astype(F32) + pr[b, r, :].astype(F32)

    for jj in range(2):
        first = 3 + 3 * jj

        def self_pair(pp, _, jj=jj, first=first):
            attend(pp, qs, ks, vt, smix, slse, qrows(jj), wide_rows * (jj + 1), True)
            at_turn(pp, 0, f"p{first}")
            at_turn(pp, 1, f"p{first + 1}")
            return 0

        lax.fori_loop(0, 2, self_pair, 0)
        for j in (2 * jj, 2 * jj + 1):
            send_sum(0, j, nt(pairs(smix, rows(j)), weight(3)))
        at(f"p{first + 2}")
    relays["m"].wait_recv()

    key_at = lax.broadcasted_iota(jnp.int32, (rows_all, LANES), 0)
    bias[...] = jnp.where(key_at < sl_ref[p], 0.0, MASKED)

    def project_cross(j, _):
        r = rows(j)
        rowsv = ms[r, :]
        put_pairs(cks, r, nn(rowsv, weight(4)))
        val = nn(rowsv, weight(5))
        put_pairs(cvs, r, val)
        put_transposed(vt, r, val.astype(BF16).astype(F32))
        return 0

    lax.fori_loop(0, 4, project_cross, 0)
    at("p9")

    def second(j, _):
        exchange(0, j).wait_recv()
        exchange(0, j).wait_send()

        def part(i, _):
            r = rows(j * per + i, sub)
            h = xs[r, :].astype(F32) + summed(0, r)
            h1[r, :] = h
            xhat, _unused = normalize(h)
            n2[r, :] = (xhat * gains[2:3, :] + gains[3:4, :]).astype(BF16)
            return 0

        lax.fori_loop(0, per, part, 0)
        r = rows(j)
        put_pairs(cqs, r, nn(n2[r, :], weight(6)).astype(BF16) * jnp.asarray(scale, BF16))
        return 0

    lax.fori_loop(0, 4, second, 0)
    at("p10")

    def cross_pair(i, _):
        jj, pp = i // 2, i % 2
        attend(pp, cqs, cks, vt, cmix, clse, qrows(jj), rows_all, False)
        for k, name in enumerate(("p11", "p12", "p14", "p15")):
            at_turn(i, k, name)

        @pl.when(pp == 1)
        def _():
            for k in range(2):
                j = 2 * jj + k
                send_sum(1, j, nt(pairs(cmix, rows(j)), weight(7)))

        at_turn(i, 1, "p13")
        return 0

    lax.fori_loop(0, 4, cross_pair, 0)
    at("p16")

    limit = tl_ref[p]

    def live(r_first, size):
        at = lax.broadcasted_iota(jnp.int32, (size, wide), 0) + r_first
        return at < limit

    def weight_grads(a_buf, items):
        chunk = ny * rb
        for zi in range(nz):
            at = a_buf[:, zi * chunk : (zi + 1) * chunk].T
            for s, load in items:
                gs[s, zi] = nn(at, load()).astype(BF16).reshape(ny, rb, 2 * LANES)

    every = pl.ds(0, rows_all)

    def whole(buf):
        return lambda: pairs(buf, every)

    def plane(buf, s):
        return lambda: buf[s]

    def reduce_part(lo, hi, first, last, order, bufs):
        r = slice(first, last)
        base = lo
        bufs = list(bufs)
        gone = []

        def at(buf, s, zsel, ysel, lsel):
            index = [s]
            if "z" not in gone:
                index.append(zsel)
            if "y" not in gone:
                index.append(ysel)
            index += [slice(None) if buf is not gs else r, lsel]
            return tuple(index)

        every_one = slice(None)
        cur, shift = gs, 0
        for hop, axis in enumerate(order):
            span = slice(lo - shift, hi - shift)
            land = bufs.pop(0)
            to = slice(lo - base, hi - base)
            lanes = every_one if "x" in gone else slice(0, 2 * LANES)
            pick = {"z": every_one, "y": every_one, "x": lanes}
            here = dict(pick)
            if axis == "x":
                pick["x"], here["x"] = other_half, half
                sends = [(pick, (land, to), x_peer)]
            elif axis == "y":
                pick["y"], here["y"] = y_other, y
                sends = [(pick, (land, to), y_peer)]
            else:
                here["z"] = z
                sends = [
                    (dict(pick, z=z_others[k - 1]), (land, (k - 1, to)), z_peer(k))
                    for k in range(1, nz)
                ]
            cps = [
                push((cur, at(cur, span, sel["z"], sel["y"], sel["x"])), dst, peer)
                for sel, dst, peer in sends
            ]
            yield
            for cp in cps:
                cp.wait_recv()
            done = hop == 2
            acc = None if done else bufs.pop(0)

            def add(s, _):
                v = cur[at(cur, s - shift, here["z"], here["y"], here["x"])].astype(F32)
                if axis == "z":
                    for k in range(1, nz):
                        v = v + land[k - 1, s - base].astype(F32)
                else:
                    v = v + land[s - base].astype(F32)
                if done:
                    gw_ref[s, r] = v
                else:
                    acc[s - base] = v.astype(BF16)
                return 0

            lax.fori_loop(lo, hi, add, 0)
            gone.append(axis)
            cur, shift = acc, base
        yield

    for name, (lo, hi) in sum_segments(nf).items():
        size = rb // len(ORDERS[name])
        tasks[name] = [
            reduce_part(lo, hi, i * size, (i + 1) * size, order, sums[name][i])
            for i, order in enumerate(ORDERS[name])
            if fused
        ]

    def third(j, _):
        exchange(1, j).wait_recv()
        exchange(1, j).wait_send()

        def part(i, _):
            r = rows(j * per + i, sub)
            h = h1[r, :] + summed(1, r)
            h2[r, :] = h
            xhat, _unused = normalize(h)
            n3[r, :] = (xhat * gains[4:5, :] + gains[5:6, :]).astype(BF16)
            return 0

        lax.fori_loop(0, per, part, 0)
        r = rows(j)
        rowsv = n3[r, :]
        for s in range(nf):
            active, slope = gelu_both(nn(rowsv, weight(8 + s)))
            act[s, r, :] = active.astype(BF16)
            gbf[s, r, :] = slope.astype(BF16)
        at_turn(j, 1, "p17")
        return 0

    lax.fori_loop(0, 4, third, 0)
    at("p18")
    relays["c"].wait_recv()

    def live_rows(i, _):
        r = rows(i, sub)
        cot = cs[r, :]
        gb16[r, :] = jnp.where(live(i * sub, sub), cot, jnp.zeros_like(cot))
        return 0

    lax.fori_loop(0, 4 * per, live_rows, 0)
    weight_grads(gb16, [(9 + nf + s, plane(act, s)) for s in range(nf)])
    at("p19")

    def third_back(j, _):
        r = rows(j)
        cot = gb16[r, :]
        for s in range(nf):
            slope = gbf[s, r, :].astype(F32)
            gbf[s, r, :] = (nn(cot, weight(8 + nf + s)) * slope).astype(BF16)
        back = nt(gbf[0, r, :], weight(8))
        for s in range(1, nf):
            back = back + nt(gbf[s, r, :], weight(8 + s))
        send_sum(2, j, back)
        val = nt(act[0, r, :], weight(8 + nf))
        for s in range(1, nf):
            val = val + nt(act[s, r, :], weight(8 + nf + s))
        ys[r, :] = val.astype(BF16)
        at_turn(j, 1, "p20")
        return 0

    lax.fori_loop(0, 4, third_back, 0)

    ycp = [
        push((ys, rows(2 * k + 1 - c)), (yr, k), core_peer) for k in range(2)
    ]

    weight_grads(n3, [(9 + s, plane(gbf, s)) for s in range(nf)])
    at("p21")

    def finish_rows(k, dst):
        def part(i, _):
            r = rows((2 * k + c) * per + i, sub)
            q = rows(i, sub)
            val = h2[r, :] + ys[r, :].astype(F32) + yr[k, q, :].astype(F32)
            keep = live(((2 * k + c) * per + i) * sub, sub)
            dst[q, :] = jnp.where(keep, val, 0.0).astype(BF16)
            return 0
        lax.fori_loop(0, per, part, 0)

    for cp in ycp:
        cp.wait_recv()
    finish_rows(1 - p, osend)
    finish_rows(p, outs.at[p])
    at("p22")

    def back_three(j, _):
        exchange(2, j).wait_recv()
        exchange(2, j).wait_send()

        def part(i, _):
            r = rows(j * per + i, sub)
            dx, dgain, dbias = norm_grad(h2[r, :], summed(2, r), gains[4:5, :])
            gacc[4:5, :] += dgain
            gacc[5:6, :] += dbias
            g = gb16[r, :].astype(F32) + dx
            gh[r, :] = g
            gb16[r, :] = g.astype(BF16)
            return 0

        return lax.fori_loop(0, per, part, 0)

    lax.fori_loop(0, 4, back_three, 0)
    weight_grads(gb16, [(7, whole(cmix))])
    at("p23")


    sel_row = lax.broadcasted_iota(jnp.int32, (8, LANES), 0)
    sel_lane = lax.broadcasted_iota(jnp.int32, (8, LANES), 1)
    selector = (sel_lane // DH == sel_row).astype(F32)

    def pair_lanes(pp):
        return pl.ds(pl.multiple_of(pp * LANES, LANES), LANES)

    def attend_back(pp, q_s, k_s, kt, v_s, mix, lse, r, keys, causal):
        parts_k = [slice(0, keys)]
        if causal and keys > wide_rows:
            parts_k = [slice(0, keys - wide_rows), slice(keys - wide_rows, keys)]

        q = q_s[pp, r, :]
        do = dm[pp, r, :]
        prod = do.astype(F32) * mix[pp, r, :].astype(F32)
        delta = lax.dot_general(
            selector, prod, (((1,), (1,)), ((), ())),
            precision=HIGHEST, preferred_element_type=F32,
        )
        back = None
        for i, kk in enumerate(parts_k):
            parts = []
            for u in range(2):
                s = nt(only(k_s[pp, kk, :], u), q)
                s = hide(s, kk.start, i == len(parts_k) - 1, causal)
                e = jnp.exp(s - lse[2 * pp + u, :, r])
                d = nt(only(v_s[pp, kk, :], u), do)
                ds = (e * (d - delta[u : u + 1])).astype(BF16)
                dv_u = nn(e.astype(BF16), only(do, u))
                dk_u = nn(ds, only(q, u))
                dvp = dv_u if u == 0 else dvp + dv_u
                dkp = dk_u if u == 0 else dkp + dk_u
                parts.append(nn(kt[pp, u * DH : (u + 1) * DH, kk], ds))
            lanes = pair_lanes(pp)
            score[0, kk, lanes] += dkp
            score[1, kk, lanes] += dvp
            parts = jnp.concatenate(parts, axis=0)
            back = parts if i == 0 else back + parts
        dq[pp, r, :] = (back * scale).T.astype(BF16)

    def transpose_keys(buf):
        def one(j, _):
            r = rows(j)
            for pp in range(2):
                vt[pp, :, r] = buf[pp, r, :].astype(F32).T.astype(BF16)
            return 0
        lax.fori_loop(0, 4, one, 0)

    transpose_keys(cks)
    score[:, :, : 2 * LANES] = jnp.zeros((2, rows_all, 2 * LANES), F32)

    def cross_back_pair(i, _):
        jj, pp = i // 2, i % 2

        @pl.when(pp == 0)
        def _():
            for k in range(2):
                r = rows(2 * jj + k)
                put_pairs(dm, r, nn(gb16[r, :], weight(7)))

        attend_back(pp, cqs, cks, vt, cvs, cmix, clse, qrows(jj), rows_all, False)
        for k in range(4):
            at_turn(i, k, f"p{24 + k}")

        @pl.when(pp == 1)
        def _():
            for k in range(2):
                j = 2 * jj + k
                send_sum(3, j, nt(pairs(dq, rows(j)), weight(6)))

        return 0

    lax.fori_loop(0, 4, cross_back_pair, 0)

    def cross_back_keys(j, _):
        r = rows(j)
        for pp in range(2):
            dk[pp, r, :] = score[0, r, pair_lanes(pp)].astype(BF16)
            dv[pp, r, :] = score[1, r, pair_lanes(pp)].astype(BF16)
        val = nt(pairs(dk, r), weight(4)) + nt(pairs(dv, r), weight(5))
        us[r, :] = val.astype(BF16)
        return 0

    lax.fori_loop(0, 4, cross_back_keys, 0)
    ucp = [
        push((us, rows(2 * k + 1 - c)), (ur, k), core_peer) for k in range(2)
    ]
    weight_grads(n2, [(6, whole(dq))])
    weight_grads(ms, [(4, whole(dk)), (5, whole(dv))])
    at("p28")

    def memory_rows(k, dst):
        def part(i, _):
            r = rows((2 * k + c) * per + i, sub)
            q = rows(i, sub)
            dst[q, :] = (us[r, :].astype(F32) + ur[k, q, :].astype(F32)).astype(BF16)
            return 0
        lax.fori_loop(0, per, part, 0)

    for cp in ucp:
        cp.wait_recv()
    memory_rows(1 - p, gmsend)
    memory_rows(p, gms.at[p])
    at("p29")

    def back_two(j, _):
        exchange(3, j).wait_recv()
        exchange(3, j).wait_send()

        def part(i, _):
            r = rows(j * per + i, sub)
            dx, dgain, dbias = norm_grad(h1[r, :], summed(3, r), gains[2:3, :])
            gacc[2:3, :] += dgain
            gacc[3:4, :] += dbias
            g = gh[r, :] + dx
            gh[r, :] = g
            gb16[r, :] = g.astype(BF16)
            return 0

        return lax.fori_loop(0, per, part, 0)

    lax.fori_loop(0, 4, back_two, 0)
    weight_grads(gb16, [(3, whole(smix))])
    at("p30")

    transpose_keys(ks)
    score[:, :, : 2 * LANES] = jnp.zeros((2, rows_all, 2 * LANES), F32)
    for jj in (1, 0):
        for j in (2 * jj, 2 * jj + 1):
            put_pairs(dm, rows(j), nn(gb16[rows(j), :], weight(3)))
        first = 33 - 2 * jj

        def self_back_pair(pp, _, jj=jj, first=first):
            attend_back(pp, qs, ks, vt, vs, smix, slse, qrows(jj), wide_rows * (jj + 1), True)
            at_turn(pp, 0, f"p{first}")
            at_turn(pp, 1, f"p{first + 1}")
            return 0

        lax.fori_loop(0, 2, self_back_pair, 0)
        for j in (2 * jj, 2 * jj + 1):
            r = rows(j)
            for pp in range(2):
                dk[pp, r, :] = score[0, r, pair_lanes(pp)].astype(BF16)
                dv[pp, r, :] = score[1, r, pair_lanes(pp)].astype(BF16)
            val = nt(pairs(dq, r), weight(0)) + nt(pairs(dk, r), weight(1))
            send_sum(4, j, val + nt(pairs(dv, r), weight(2)))

    weight_grads(n1, [(0, whole(dq)), (1, whole(dk)), (2, whole(dv))])
    at("p35")

    def back_one(k, j, dst):
        exchange(4, j).wait_recv()

        def part(i, _):
            r = rows(j * per + i, sub)
            q = rows(i, sub)
            dx, dgain, dbias = norm_grad(xs[r, :].astype(F32), summed(4, r), gains[0:1, :])
            gacc[0:1, :] += dgain
            gacc[1:2, :] += dbias
            if dst is not None:
                dst[q, :] = (gh[r, :] + dx).astype(BF16)
            return 0

        lax.fori_loop(0, per, part, 0)

    back_one(0, tx, gisend)
    at("p36")
    back_one(0, t, gis.at[p])
    back_one(0, 2 * p + 1 - c, None)
    back_one(0, 2 * (1 - p) + 1 - c, None)
    for j in range(4):
        exchange(4, j).wait_send()

    spread_rows = jnp.concatenate(
        [gacc[...], jnp.zeros((LANES - 8, wide), F32)], axis=0
    )
    columns = spread_rows.T.astype(BF16)
    gs[gseg] = jnp.concatenate([columns, columns], axis=1).reshape(nz, ny, rb, 2 * LANES)

    at("p37")
    last = [] if fused else [local((gs, None), (gw_ref, None))]

    finals = [
        local((outs, None), (out_ref, None)),
        local((gms, None), (gm_ref, None)),
        local((gis, None), (gi_ref, None)),
    ]
    for cp in finals + last:
        cp.wait()
    for cp in sent:
        cp.copy().wait_send()


def unpack_kernel(nf, o_ref, gi_ref, gm_ref, gw_ref, *outs):
    outs[0][...] = o_ref[...]
    outs[1][...] = gi_ref[...].astype(F32)
    outs[2][...] = gm_ref[...].astype(F32)
    outs[3][...] = gw_ref[0:3]
    outs[4][...] = gw_ref[3]
    outs[5][...] = gw_ref[6]
    outs[6][...] = gw_ref[4:6]
    outs[7][...] = gw_ref[7]
    for i in range(nf):
        outs[8][:, i * LANES : (i + 1) * LANES] = gw_ref[9 + i]
        outs[9][:, i * LANES : (i + 1) * LANES] = gw_ref[9 + nf + i]
    vectors = gw_ref[8].T
    for i in range(6):
        outs[10 + i][...] = vectors[i : i + 1]


def body(ndp, inputs, memory, tgt_len, src_len, cotangent, w_qkv, w_out, cross_query, cross_kv,
         cross_out, ffn_up, ffn_down, *gain_list):
    own, wide = inputs.shape[1], inputs.shape[2]
    rb = w_qkv.shape[1]
    nf = ffn_up.shape[1] // LANES
    nseg = 8 + 2 * nf
    rows_all = 4 * own
    fused = rb % 32 == 0 and ndp % 2 == 0
    if fused:
        ny, nz, block = 2, ndp // 2, rb
    else:
        ny, nz, block = 1, 1, wide
    cfg = (fused, nz, ny, block, own, wide, nf)

    any_spec = pl.BlockSpec(memory_space=pl.ANY)
    smem = pl.BlockSpec(memory_space=pltpu.SMEM)
    vmem = pl.BlockSpec(memory_space=pltpu.VMEM)
    operands = [inputs, memory, cotangent, tgt_len, src_len]
    specs = [any_spec] * 3 + [smem] * 2
    if fused:
        weights = [w_qkv, w_out.T, cross_query, cross_kv, cross_out.T, ffn_up, ffn_down.T]
        weights += [g[None, :] for g in gain_list]
        operands += weights
        specs += [vmem] * len(weights)
    else:
        pieces = [w_qkv, w_out.T[None], cross_kv, cross_query[None], cross_out.T[None]]
        pieces += [ffn_up.reshape(rb, nf, LANES).swapaxes(0, 1)]
        pieces += [ffn_down.reshape(nf, LANES, rb).swapaxes(1, 2)]
        packed = lax.all_gather(jnp.concatenate(pieces, axis=0), "dp", axis=1, tiled=True)
        index = lax.axis_index("tensor")
        flipped = lax.ppermute(packed, "tensor", [(i, (i + 2) % 4) for i in range(4)])
        low = jnp.where(index < 2, packed, flipped)
        high = jnp.where(index < 2, flipped, packed)
        full = jnp.concatenate([low, high], axis=2)[:, None, None]
        gathered = lax.all_gather(jnp.stack(gain_list), "dp", axis=1, tiled=True)
        operands += [full, jnp.pad(gathered.astype(F32), ((0, 10), (0, 0)))]
        specs += [any_spec, vmem]

    bf = lambda *shape: pltpu.VMEM(shape, BF16)
    fl = lambda *shape: pltpu.VMEM(shape, F32)
    seq = (rows_all, wide)
    heads = (2, rows_all, LANES)
    scratch = [
        bf(*seq), bf(*seq), bf(*seq), bf(nseg, nz, ny, block, 2 * LANES), fl(16, wide),
        bf(*seq), bf(*seq), bf(*seq), fl(*seq), fl(*seq), fl(*seq), bf(*seq),
        bf(*heads), bf(*heads), bf(*heads), bf(*heads), bf(*heads), bf(*heads),
        bf(2, LANES, rows_all), bf(*heads), bf(*heads), fl(4, 1, rows_all), fl(4, 1, rows_all),
        bf(nf, rows_all, 2 * LANES), bf(nf, rows_all, 2 * LANES),
        bf(*heads), bf(*heads), bf(*heads), bf(*heads),
        bf(2, *seq), bf(2, *seq), bf(*seq), bf(2, own, wide), bf(*seq), bf(2, own, wide),
        bf(2, own, wide), bf(own, wide), bf(2, own, wide), bf(own, wide),
        bf(2, own, wide), bf(own, wide),
        bf(nseg + 1, nz, ny, block, 2 * LANES), fl(rows_all, LANES), fl(8, wide),
        fl(2, rows_all, 2 * own),
    ]
    if fused:
        scratch += [bf(nz, 16, wide), bf(2, 16, wide)]
        for name, (lo, hi) in sum_segments(nf).items():
            for order in ORDERS[name]:
                shapes = sum_shapes(order, hi - lo, nz, ny, block // len(ORDERS[name]))
                scratch += [bf(*shape) for shape in shapes]
    dma = pltpu.SemaphoreType.DMA
    scratch += [dma((250,)), dma((250,)), dma((20,)), dma((20,)), dma((12,))]

    if fused:
        grads_shape = jax.ShapeDtypeStruct((nseg + 1, block, LANES), F32)
        grads_spec = vmem
    else:
        grads_shape = jax.ShapeDtypeStruct((nseg + 1, nz, ny, block, 2 * LANES), BF16)
        grads_spec = any_spec
    act_shape = jax.ShapeDtypeStruct(inputs.shape, BF16)
    output, grad_in, grad_mem, grads = pl.pallas_call(
        functools.partial(layer_kernel, cfg),
        out_shape=(act_shape, act_shape, act_shape, grads_shape),
        in_specs=specs,
        out_specs=(any_spec, any_spec, any_spec, grads_spec),
        scratch_shapes=scratch,
        compiler_params=pltpu.CompilerParams(
            collective_id=0, has_side_effects=True, vmem_limit_bytes=62 << 20
        ),
        name="layer",
    )(*operands)

    if not fused:
        mine = grads[:, 0, 0].astype(F32)
        index = lax.axis_index("tensor")
        low, high = mine[:, :, :LANES], mine[:, :, LANES:]
        keep = jnp.where(index < 2, low, high)
        give = jnp.where(index < 2, high, low)
        keep = keep + lax.ppermute(give, "tensor", [(i, (i + 2) % 4) for i in range(4)])
        grads = lax.psum_scatter(keep, "dp", scatter_dimension=1, tiled=True)

    shapes = [
        (inputs.shape, BF16), (inputs.shape, F32), (memory.shape, F32),
        (w_qkv.shape, F32), (w_out.shape[::-1], F32), (cross_query.shape, F32),
        (cross_kv.shape, F32), (cross_out.shape[::-1], F32), (ffn_up.shape, F32),
        (ffn_down.shape[::-1], F32),
    ] + [((1, rb), F32)] * 6
    got = pl.pallas_call(
        functools.partial(unpack_kernel, nf),
        out_shape=[jax.ShapeDtypeStruct(*s) for s in shapes],
        in_specs=[vmem] * 4,
        out_specs=[vmem] * len(shapes),
        name="unpack",
    )(output, grad_in, grad_mem, grads)
    return (
        *got[:4], got[4].T, got[5], got[6], got[7].T, got[8], got[9].T,
        *[g[0] for g in got[10:]],
    )


def solution(mesh):
    return jax.shard_map(
        functools.partial(body, mesh.shape["dp"]),
        mesh=mesh,
        in_specs=(
            P("dp", "tensor", None),
            P("dp", "tensor", None),
            P("dp"),
            P("dp"),
            P("dp", "tensor", None),
            P(None, "dp", "tensor"),
            P("tensor", "dp"),
            P("dp", "tensor"),
            P(None, "dp", "tensor"),
            P("tensor", "dp"),
            P("dp", "tensor"),
            P("tensor", "dp"),
            P("dp"),
            P("dp"),
            P("dp"),
            P("dp"),
            P("dp"),
            P("dp"),
        ),
        out_specs=(
            P("dp", "tensor", None),
            P("dp", "tensor", None),
            P("dp", "tensor", None),
            P(None, "dp", "tensor"),
            P("tensor", "dp"),
            P("dp", "tensor"),
            P(None, "dp", "tensor"),
            P("tensor", "dp"),
            P("dp", "tensor"),
            P("tensor", "dp"),
            P("dp"),
            P("dp"),
            P("dp"),
            P("dp"),
            P("dp"),
            P("dp"),
        ),
        check_vma=False,
    )
```

profile of v0, /device:TPU:0, one launch (start us, length us, event | category | flops | bytes accessed | tf_op | source)
XLA Modules:
  0.0 138.6 jit_solution(4258878914822414479)
XLA Ops:
  0.7 134.5 %layer.1 = (bf16[2,256,512]{2,1,0:T(8,128)(2,1)}, bf16[2,256,512]{2,1,0:T(8,128)(2,1)}, bf16[2,256,512]{2,1,0:T(8,128)(2,1)}, f32[17,64,128]{2,1,0:T(8,128)}) custom-call(bf16[2,256,512]{2,1,0:T(8,128)(2,1)} %refs_0_.1, bf16[2,256,512]{2,1,0:T(8,128)(2,1)} %refs_1_.1, bf16[2,256,512]{2,1,0:T(8,128)(2,1)} %refs_2_.1, s32[2]{0:T(128)} %refs_3_.1, s32[2]{0:T(128)} %refs_4_.1, ...), custom_call_target="tpu_custom_call" | custom-call | tf_op jit(solution)/shard_map/layer/pallas_call | solution.py:1026
  135.2 3.3 %unpack.1 = (bf16[2,256,512]{2,1,0:T(8,128)(2,1)}, f32[2,256,512]{2,1,0:T(8,128)}, f32[2,256,512]{2,1,0:T(8,128)}, f32[3,64,128]{2,1,0:T(8,128)}, f32[64,128]{1,...) custom-call(bf16[2,256,512]{2,1,0:T(8,128)(2,1)} %get-tuple-element., ...), custom_call_target="tpu_custom_call" | custom-call | tf_op jit(solution)/shard_map/unpack/pallas_call | solution.py:1053
where the time goes:
time: 139 us
  Pallas kernels  138 us (99%)
    pallas_call x1, Pallas kernels, body(): pl.pallas_call(functools.partial(layer_kernel, cfg), out_shape=(act_shape...  134 us
    pallas_call x1, Pallas kernels, body(): pl.pallas_call(functools.partial(unpack_kernel, nf), out_shape=[jax.Shape...  3.3 us

commit v1 on v0

--- a/solution.py
+++ b/solution.py
@@ -378,7 +378,7 @@
     if not fused:
         wcp.wait()
 
-    sub = min(64, own)
+    sub = min(128, own)
     per = own // sub
     gacc[...] = jnp.zeros_like(gacc)
 

time: 139 us -> 133 us (0.957)
  Pallas kernels: 138 us -> 131 us
    pallas_call x1, Pallas kernels: 134 us -> 128 us  [body(): pl.pallas_call(functools.partial(layer_kernel, cfg), out_shape=(act_shape...]
where the time goes in v1:
time: 133 us; the launch traced here: 132 us
  Pallas kernels  131 us (98%)
    pallas_call x1, Pallas kernels, body(): pl.pallas_call(functools.partial(layer_kernel, cfg), out_shape=(act_shape...  128 us
    pallas_call x1, Pallas kernels, body(): pl.pallas_call(functools.partial(unpack_kernel, nf), out_shape=[jax.Shape...  3.3 us

profile of v1, /device:TPU:0, one launch (start us, length us, event | category | flops | bytes accessed | tf_op | source)
XLA Modules:
  0.0 132.3 jit_solution(15753253451010090342)
XLA Ops:
  0.7 128.2 %layer.1 = (bf16[2,256,512]{2,1,0:T(8,128)(2,1)}, bf16[2,256,512]{2,1,0:T(8,128)(2,1)}, bf16[2,256,512]{2,1,0:T(8,128)(2,1)}, f32[17,64,128]{2,1,0:T(8,128)}) custom-call(bf16[2,256,512]{2,1,0:T(8,128)(2,1)} %refs_0_.1, bf16[2,256,512]{2,1,0:T(8,128)(2,1)} %refs_1_.1, bf16[2,256,512]{2,1,0:T(8,128)(2,1)} %refs_2_.1, s32[2]{0:T(128)} %refs_3_.1, s32[2]{0:T(128)} %refs_4_.1, ...), custom_call_target="tpu_custom_call" | custom-call | tf_op jit(solution)/shard_map/layer/pallas_call | solution.py:1026
  128.8 3.3 %unpack.1 = (bf16[2,256,512]{2,1,0:T(8,128)(2,1)}, f32[2,256,512]{2,1,0:T(8,128)}, f32[2,256,512]{2,1,0:T(8,128)}, f32[3,64,128]{2,1,0:T(8,128)}, f32[64,128]{1,...) custom-call(bf16[2,256,512]{2,1,0:T(8,128)(2,1)} %get-tuple-element., ...), custom_call_target="tpu_custom_call" | custom-call | tf_op jit(solution)/shard_map/unpack/pallas_call | solution.py:1053

commit v2 on v1

--- a/solution.py
+++ b/solution.py
@@ -391,6 +391,11 @@
     lax.fori_loop(0, 4 * per, norm_rows, 0)
     at("p1")
 
+    wide_rows = 2 * own
+
+    def qrows(jj):
+        return pl.ds(pl.multiple_of(jj * wide_rows, wide_rows), wide_rows)
+
     def put_pairs(buf, r, value):
         v = value.astype(BF16)
         buf[0, r, :] = v[:, :LANES]
@@ -407,7 +412,7 @@
         buf[1, :, r] = vt_[LANES:]
 
     def project(j, _):
-        r = rows(j)
+        r = qrows(j)
         rowsv = n1[r, :]
         put_pairs(qs, r, nn(rowsv, weight(0)).astype(BF16) * jnp.asarray(scale, BF16))
         put_pairs(ks, r, nn(rowsv, weight(1)))
@@ -416,7 +421,7 @@
         put_transposed(vt, r, val.astype(BF16).astype(F32))
         return 0
 
-    lax.fori_loop(0, 4, project, 0)
+    lax.fori_loop(0, 2, project, 0)
     at("p2")
 
 
@@ -425,11 +430,6 @@
 
     def only(value, u):
         return value * head_lanes[u]
-
-    wide_rows = 2 * own
-
-    def qrows(jj):
-        return pl.ds(pl.multiple_of(jj * wide_rows, wide_rows), wide_rows)
 
     def hide(scores, first, diagonal, causal):
         if causal and not diagonal:
@@ -501,7 +501,7 @@
     bias[...] = jnp.where(key_at < sl_ref[p], 0.0, MASKED)
 
     def project_cross(j, _):
-        r = rows(j)
+        r = qrows(j)
         rowsv = ms[r, :]
         put_pairs(cks, r, nn(rowsv, weight(4)))
         val = nn(rowsv, weight(5))
@@ -509,7 +509,7 @@
         put_transposed(vt, r, val.astype(BF16).astype(F32))
         return 0
 
-    lax.fori_loop(0, 4, project_cross, 0)
+    lax.fori_loop(0, 2, project_cross, 0)
     at("p9")
 
     def second(j, _):
@@ -644,28 +644,29 @@
         ]
 
     def third(j, _):
-        exchange(1, j).wait_recv()
-        exchange(1, j).wait_send()
+        for k in range(2):
+            exchange(1, 2 * j + k).wait_recv()
+            exchange(1, 2 * j + k).wait_send()
 
         def part(i, _):
-            r = rows(j * per + i, sub)
+            r = rows(2 * j * per + i, sub)
             h = h1[r, :] + summed(1, r)
             h2[r, :] = h
             xhat, _unused = normalize(h)
             n3[r, :] = (xhat * gains[4:5, :] + gains[5:6, :]).astype(BF16)
             return 0
 
-        lax.fori_loop(0, per, part, 0)
-        r = rows(j)
+        lax.fori_loop(0, 2 * per, part, 0)
+        r = qrows(j)
         rowsv = n3[r, :]
         for s in range(nf):
             active, slope = gelu_both(nn(rowsv, weight(8 + s)))
             act[s, r, :] = active.astype(BF16)
             gbf[s, r, :] = slope.astype(BF16)
-        at_turn(j, 1, "p17")
+        at_turn(j, 0, "p17")
         return 0
 
-    lax.fori_loop(0, 4, third, 0)
+    lax.fori_loop(0, 2, third, 0)
     at("p18")
     relays["c"].wait_recv()
 
@@ -680,7 +681,7 @@
     at("p19")
 
     def third_back(j, _):
-        r = rows(j)
+        r = qrows(j)
         cot = gb16[r, :]
         for s in range(nf):
             slope = gbf[s, r, :].astype(F32)
@@ -688,15 +689,16 @@
         back = nt(gbf[0, r, :], weight(8))
         for s in range(1, nf):
             back = back + nt(gbf[s, r, :], weight(8 + s))
-        send_sum(2, j, back)
+        for k in range(2):
+            send_sum(2, 2 * j + k, back[k * own : (k + 1) * own])
         val = nt(act[0, r, :], weight(8 + nf))
         for s in range(1, nf):
             val = val + nt(act[s, r, :], weight(8 + nf + s))
         ys[r, :] = val.astype(BF16)
-        at_turn(j, 1, "p20")
+        at_turn(j, 0, "p20")
         return 0
 
-    lax.fori_loop(0, 4, third_back, 0)
+    lax.fori_loop(0, 2, third_back, 0)
 
     ycp = [
         push((ys, rows(2 * k + 1 - c)), (yr, k), core_peer) for k in range(2)

time: 133 us -> 132 us (level)
  no operation moved by 1% of the time
where the time goes in v2:
time: 132 us
  Pallas kernels  131 us (99%)
    pallas_call x1, Pallas kernels, body(): pl.pallas_call(functools.partial(layer_kernel, cfg), out_shape=(act_shape...  128 us
    pallas_call x1, Pallas kernels, body(): pl.pallas_call(functools.partial(unpack_kernel, nf), out_shape=[jax.Shape...  3.3 us

profile of v2, /device:TPU:0, one launch (start us, length us, event | category | flops | bytes accessed | tf_op | source)
XLA Modules:
  0.0 132.2 jit_solution(3480546600903547981)
XLA Ops:
  0.7 128.1 %layer.1 = (bf16[2,256,512]{2,1,0:T(8,128)(2,1)}, bf16[2,256,512]{2,1,0:T(8,128)(2,1)}, bf16[2,256,512]{2,1,0:T(8,128)(2,1)}, f32[17,64,128]{2,1,0:T(8,128)}) custom-call(bf16[2,256,512]{2,1,0:T(8,128)(2,1)} %refs_0_.1, bf16[2,256,512]{2,1,0:T(8,128)(2,1)} %refs_1_.1, bf16[2,256,512]{2,1,0:T(8,128)(2,1)} %refs_2_.1, s32[2]{0:T(128)} %refs_3_.1, s32[2]{0:T(128)} %refs_4_.1, ...), custom_call_target="tpu_custom_call" | custom-call | tf_op jit(solution)/shard_map/layer/pallas_call | solution.py:1028
  128.8 3.3 %unpack.1 = (bf16[2,256,512]{2,1,0:T(8,128)(2,1)}, f32[2,256,512]{2,1,0:T(8,128)}, f32[2,256,512]{2,1,0:T(8,128)}, f32[3,64,128]{2,1,0:T(8,128)}, f32[64,128]{1,...) custom-call(bf16[2,256,512]{2,1,0:T(8,128)(2,1)} %get-tuple-element., ...), custom_call_target="tpu_custom_call" | custom-call | tf_op jit(solution)/shard_map/unpack/pallas_call | solution.py:1055
